TPU v7x, 512 devices: a whole 4x4x16 slice. The times are simulated.
512 devices in a mesh: dp: 16 (over z_hi, y), tensor: 32 (over z_lo, x, core).
Axes of the slice: x: 4, y: 4, z: 16 (z_hi: 4, z_lo: 4; z = z_hi * 4 + z_lo), core: 2. Of those that a mesh axis runs over, the one named last changes fastest.
Arguments:
- hidden: bfloat16 [1024, 32, 28672], P('dp', None, 'tensor'), may hold values from -6 to 6
- out_grad: bfloat16 [1024, 32, 8192], P('dp', None, 'tensor'), may hold values from -6 to 6
- proj_in: bfloat16 [28672, 64], P('tensor'), may hold values from -0.03125 to 0.03125
- proj_out: bfloat16 [8192, 64], P('tensor'), may hold values from -0.0625 to 0.0625
- lengths: int32 [1024], P('dp'), may hold values from 1 to 32, 16384 in all
- task_ids: int32 [16], replicated, may hold values from 0 to 1
Outputs:
- similarity: float32 [1024, 16, 64], P('dp', None, 'tensor')
Inputs may be any that keep to these rules, and one draw needn't show every extreme that they name: `lengths`: at least one sequence is exactly 32 long.
All inputs are finite; a program needn't handle non-finite values. No bound on the sum of `lengths` on one device may be relied on, other than what follows from the above.
Results may differ from a plain program's by a relative error of at most 0.0003.
Values sent between devices are 32-bit elements; how exact they have to be, the bound alone decides.
No kernel may reach another device: no remote copies, remote signals or barrier semaphores. Data moves between devices by JAX's collectives and lax.ppermute only.
A program may use at most 64 MiB of HBM per device.

v0:
```python
import jax
import jax.numpy as jnp
from jax import lax
from jax.sharding import PartitionSpec as P

epsilon = 1e-06


def from_behind(value, axis, steps):
    count = lax.axis_size(axis)
    pairs = [(source, (source + steps) % count) for source in range(count)]
    return lax.ppermute(value, axis, pairs)


def normalized(summed, lengths):
    seq_count, seq_len, doubled = summed.shape
    width_low = doubled // 2
    live_mask = (jnp.arange(seq_len, dtype=jnp.int32)[None, :] < lengths[:, None]).astype(
        jnp.float32
    )
    inputs_low = summed[:, :, :width_low] * live_mask[:, :, None]
    outputs_low = summed[:, :, width_low:]
    sketch = jnp.einsum("slk,slm->skm", inputs_low, outputs_low, precision=lax.Precision.HIGHEST)
    flattened = sketch.reshape(seq_count, width_low * width_low)
    root_mean = jnp.sqrt(jnp.mean(flattened * flattened, axis=1, keepdims=True) + epsilon)
    return flattened / root_mean


def inner_rows(left, right):
    return lax.dot_general(
        left,
        right,
        (((1,), (1,)), ((), ())),
        preferred_element_type=jnp.float32,
        precision=lax.Precision.HIGHEST,
    )


def body(hidden, out_grad, proj_in, proj_out, lengths, task_ids):
    block_rows, seq_len, _ = hidden.shape
    groups = lax.axis_size("dp")
    slices = lax.axis_size("tensor")
    share_rows = block_rows // slices
    group_index = lax.axis_index("dp")
    slice_index = lax.axis_index("tensor")
    width_low = proj_in.shape[1]
    factor = 1.0 / width_low
    inputs_part = jnp.dot(
        hidden.reshape(block_rows * seq_len, -1), proj_in, preferred_element_type=jnp.float32
    )
    outputs_part = jnp.dot(
        out_grad.reshape(block_rows * seq_len, -1), proj_out, preferred_element_type=jnp.float32
    )
    partial_value = jnp.concatenate([inputs_part, outputs_part], axis=1).reshape(
        block_rows, seq_len, 2 * width_low
    )
    summed = lax.psum(partial_value, "tensor")
    own_block = normalized(summed, lengths)
    mine = lax.dynamic_slice_in_dim(own_block, slice_index * share_rows, share_rows, 0)
    block_ids = jnp.arange(groups, dtype=jnp.int32)
    own_task = jnp.sum(jnp.where(block_ids == group_index, task_ids, 0))

    def place(result, visiting, source):
        source_task = jnp.sum(jnp.where(block_ids == source, task_ids, 0))
        product = inner_rows(own_block, visiting)
        piece = jnp.where(own_task == source_task, product * factor, jnp.float32(0.0))
        starts = (jnp.int32(0), source, jnp.int32(0))
        return lax.dynamic_update_slice(result, piece[:, None, :], starts)

    result = jnp.zeros((block_rows, groups, share_rows), jnp.float32)
    result = place(result, mine, group_index)

    def advance(offset, carried):
        visiting, result = carried
        visiting = from_behind(visiting, "dp", 1)
        source = (group_index - offset) % groups
        return (visiting, place(result, visiting, source))

    _, result = lax.fori_loop(1, groups, advance, (mine, result))
    return result


def solution(mesh):
    in_specs = (
        P("dp", None, "tensor"),
        P("dp", None, "tensor"),
        P("tensor", None),
        P("tensor", None),
        P("dp"),
        P(),
    )
    out_specs = P("dp", None, "tensor")
    return jax.shard_map(body, mesh=mesh, in_specs=in_specs, out_specs=out_specs, check_vma=False)
```

profile of v0, /device:TPU:128, one launch (start us, length us, event | category | flops | bytes accessed | tf_op | source)
XLA Modules:
  0.0 518.5 jit_solution(16584083541157340473)
XLA Ops:
  8.9 3.3 fusion.13
  14.5 292.5 %all-reduce.2.cloned.1.call-done = f32[64,32,128]{2,1,0:T(8,128)} async-done(((f32[64,32,128]{2,1,0:T(8,128)}), f32[64,32,128]{2,1,0:T(8,128)}) %all-reduce.2.cloned.1.call-update) | async-done | bytes 1048592 | tf_op jit(solution)/shard_map/psum | solution.py:57
  307.0 6.2 %multiply_reduce_fusion = (f32[64]{0:T(128)S(1)}, f32[64,64,64]{2,1,0:T(8,128)S(1)}) fusion(f32[64,32,128]{2,1,0:T(8,128)} %all-reduce.2.cloned.1.call-done, f32[64,32]{1,0:T(8,128)S(1)} %fusion.11), kind=kOutput, calls=%fused_computation.7 | convolution fusion | flops 101318592 | bytes 3154176 | tf_op jit(solution)/shard_map/slk,slm->skm/dot_general | solution.py:23
  317.2 193.9 %while.18 = (s32[]{:T(128)}, f32[2,4096]{1,0:T(2,128)S(1)}, f32[64,16,2]{0,2,1:T(2,128)S(1)}, s32[]{:T(128)}, s32[16]{0:T(128)S(1)}, /*index=5*/s32[]{:T(128)}, ...) while((s32[]{:T(128)}, f32[2,4096]{1,0:T(2,128)S(1)}, ...), condition=%wide.region_5.6_spmd.clone, body=%wide.region_3.0_spmd.clone.sunk | while | flops 6291777 | bytes 1279366 | solution.py:79
  317.2 3.4 collective-permute-start
  322.7 7.5 %collective-permute-done = f32[2,4096]{1,0:T(2,128)S(1)} collective-permute-done((f32[2,4096]{1,0:T(2,128)S(1)}, f32[2,4096]{1,0:T(2,128)S(1)}, u32[]{:S(2)}, u32[]{:S(2)}) %collective-permute-start) | collective-permute-done | bytes 32800 | tf_op jit(solution)/shard_map/while/body/eval_jaxpr/ppermute | solution.py:12
  335.1 8.0 %collective-permute-done = f32[2,4096]{1,0:T(2,128)S(1)} collective-permute-done((f32[2,4096]{1,0:T(2,128)S(1)}, f32[2,4096]{1,0:T(2,128)S(1)}, u32[]{:S(2)}, u32[]{:S(2)}) %collective-permute-start) | collective-permute-done | bytes 32800 | tf_op jit(solution)/shard_map/while/body/eval_jaxpr/ppermute | solution.py:12
  348.0 8.0 %collective-permute-done = f32[2,4096]{1,0:T(2,128)S(1)} collective-permute-done((f32[2,4096]{1,0:T(2,128)S(1)}, f32[2,4096]{1,0:T(2,128)S(1)}, u32[]{:S(2)}, u32[]{:S(2)}) %collective-permute-start) | collective-permute-done | bytes 32800 | tf_op jit(solution)/shard_map/while/body/eval_jaxpr/ppermute | solution.py:12
  360.9 8.3 %collective-permute-done = f32[2,4096]{1,0:T(2,128)S(1)} collective-permute-done((f32[2,4096]{1,0:T(2,128)S(1)}, f32[2,4096]{1,0:T(2,128)S(1)}, u32[]{:S(2)}, u32[]{:S(2)}) %collective-permute-start) | collective-permute-done | bytes 32800 | tf_op jit(solution)/shard_map/while/body/eval_jaxpr/ppermute | solution.py:12
  374.1 7.9 %collective-permute-done = f32[2,4096]{1,0:T(2,128)S(1)} collective-permute-done((f32[2,4096]{1,0:T(2,128)S(1)}, f32[2,4096]{1,0:T(2,128)S(1)}, u32[]{:S(2)}, u32[]{:S(2)}) %collective-permute-start) | collective-permute-done | bytes 32800 | tf_op jit(solution)/shard_map/while/body/eval_jaxpr/ppermute | solution.py:12
  386.9 7.9 %collective-permute-done = f32[2,4096]{1,0:T(2,128)S(1)} collective-permute-done((f32[2,4096]{1,0:T(2,128)S(1)}, f32[2,4096]{1,0:T(2,128)S(1)}, u32[]{:S(2)}, u32[]{:S(2)}) %collective-permute-start) | collective-permute-done | bytes 32800 | tf_op jit(solution)/shard_map/while/body/eval_jaxpr/ppermute | solution.py:12
  399.6 8.3 %collective-permute-done = f32[2,4096]{1,0:T(2,128)S(1)} collective-permute-done((f32[2,4096]{1,0:T(2,128)S(1)}, f32[2,4096]{1,0:T(2,128)S(1)}, u32[]{:S(2)}, u32[]{:S(2)}) %collective-permute-start) | collective-permute-done | bytes 32800 | tf_op jit(solution)/shard_map/while/body/eval_jaxpr/ppermute | solution.py:12
  412.8 8.0 %collective-permute-done = f32[2,4096]{1,0:T(2,128)S(1)} collective-permute-done((f32[2,4096]{1,0:T(2,128)S(1)}, f32[2,4096]{1,0:T(2,128)S(1)}, u32[]{:S(2)}, u32[]{:S(2)}) %collective-permute-start) | collective-permute-done | bytes 32800 | tf_op jit(solution)/shard_map/while/body/eval_jaxpr/ppermute | solution.py:12
  421.7 1.9 collective-permute-start
  425.6 7.9 %collective-permute-done = f32[2,4096]{1,0:T(2,128)S(1)} collective-permute-done((f32[2,4096]{1,0:T(2,128)S(1)}, f32[2,4096]{1,0:T(2,128)S(1)}, u32[]{:S(2)}, u32[]{:S(2)}) %collective-permute-start) | collective-permute-done | bytes 32800 | tf_op jit(solution)/shard_map/while/body/eval_jaxpr/ppermute | solution.py:12
  438.4 8.0 %collective-permute-done = f32[2,4096]{1,0:T(2,128)S(1)} collective-permute-done((f32[2,4096]{1,0:T(2,128)S(1)}, f32[2,4096]{1,0:T(2,128)S(1)}, u32[]{:S(2)}, u32[]{:S(2)}) %collective-permute-start) | collective-permute-done | bytes 32800 | tf_op jit(solution)/shard_map/while/body/eval_jaxpr/ppermute | solution.py:12
  447.3 1.9 collective-permute-start
  451.3 7.9 %collective-permute-done = f32[2,4096]{1,0:T(2,128)S(1)} collective-permute-done((f32[2,4096]{1,0:T(2,128)S(1)}, f32[2,4096]{1,0:T(2,128)S(1)}, u32[]{:S(2)}, u32[]{:S(2)}) %collective-permute-start) | collective-permute-done | bytes 32800 | tf_op jit(solution)/shard_map/while/body/eval_jaxpr/ppermute | solution.py:12
  460.0 1.9 collective-permute-start
  464.0 7.9 %collective-permute-done = f32[2,4096]{1,0:T(2,128)S(1)} collective-permute-done((f32[2,4096]{1,0:T(2,128)S(1)}, f32[2,4096]{1,0:T(2,128)S(1)}, u32[]{:S(2)}, u32[]{:S(2)}) %collective-permute-start) | collective-permute-done | bytes 32800 | tf_op jit(solution)/shard_map/while/body/eval_jaxpr/ppermute | solution.py:12
  476.8 7.9 %collective-permute-done = f32[2,4096]{1,0:T(2,128)S(1)} collective-permute-done((f32[2,4096]{1,0:T(2,128)S(1)}, f32[2,4096]{1,0:T(2,128)S(1)}, u32[]{:S(2)}, u32[]{:S(2)}) %collective-permute-start) | collective-permute-done | bytes 32800 | tf_op jit(solution)/shard_map/while/body/eval_jaxpr/ppermute | solution.py:12
  489.5 7.9 %collective-permute-done = f32[2,4096]{1,0:T(2,128)S(1)} collective-permute-done((f32[2,4096]{1,0:T(2,128)S(1)}, f32[2,4096]{1,0:T(2,128)S(1)}, u32[]{:S(2)}, u32[]{:S(2)}) %collective-permute-start) | collective-permute-done | bytes 32800 | tf_op jit(solution)/shard_map/while/body/eval_jaxpr/ppermute | solution.py:12
  498.3 1.9 collective-permute-start
  502.3 7.9 %collective-permute-done = f32[2,4096]{1,0:T(2,128)S(1)} collective-permute-done((f32[2,4096]{1,0:T(2,128)S(1)}, f32[2,4096]{1,0:T(2,128)S(1)}, u32[]{:S(2)}, u32[]{:S(2)}) %collective-permute-start) | collective-permute-done | bytes 32800 | tf_op jit(solution)/shard_map/while/body/eval_jaxpr/ppermute | solution.py:12
  (76 shorter events, 53.1 us)
Async XLA Ops:
  6.5 1.2 copy-start
  6.5 300.5 %all-reduce.2.cloned.1.call-start = ((), (), s32[]{:S(2)}) async-start(), calls=%async_computation | async-start | bytes 2097152 | tf_op jit(solution)/shard_map/psum | solution.py:57
  12.2 1.5 copy-start.3
  12.2 2.2 copy-start.2
  317.2 13.0 %collective-permute-start = (f32[2,4096]{1,0:T(2,128)S(1)}, f32[2,4096]{1,0:T(2,128)S(1)}, u32[]{:S(2)}, u32[]{:S(2)}) collective-permute-start(f32[2,4096]{1,0:T(2,128)S(1)} %get-tuple-element.292), channel_id=1, source_target_pairs={{0,32},{32,64},{64,96},{96,128},{128,160},{160,192},{192,224},{224... | collective-permute-start | bytes 98312 | tf_op jit(solution)/shard_map/while/body/eval_jaxpr/ppermute | solution.py:12
  331.1 12.0 %collective-permute-start = (f32[2,4096]{1,0:T(2,128)S(1)}, f32[2,4096]{1,0:T(2,128)S(1)}, u32[]{:S(2)}, u32[]{:S(2)}) collective-permute-start(f32[2,4096]{1,0:T(2,128)S(1)} %get-tuple-element.292), channel_id=1, source_target_pairs={{0,32},{32,64},{64,96},{96,128},{128,160},{160,192},{192,224},{224... | collective-permute-start | bytes 98312 | tf_op jit(solution)/shard_map/while/body/eval_jaxpr/ppermute | solution.py:12
  344.0 12.0 %collective-permute-start = (f32[2,4096]{1,0:T(2,128)S(1)}, f32[2,4096]{1,0:T(2,128)S(1)}, u32[]{:S(2)}, u32[]{:S(2)}) collective-permute-start(f32[2,4096]{1,0:T(2,128)S(1)} %get-tuple-element.292), channel_id=1, source_target_pairs={{0,32},{32,64},{64,96},{96,128},{128,160},{160,192},{192,224},{224... | collective-permute-start | bytes 98312 | tf_op jit(solution)/shard_map/while/body/eval_jaxpr/ppermute | solution.py:12
  356.9 12.2 %collective-permute-start = (f32[2,4096]{1,0:T(2,128)S(1)}, f32[2,4096]{1,0:T(2,128)S(1)}, u32[]{:S(2)}, u32[]{:S(2)}) collective-permute-start(f32[2,4096]{1,0:T(2,128)S(1)} %get-tuple-element.292), channel_id=1, source_target_pairs={{0,32},{32,64},{64,96},{96,128},{128,160},{160,192},{192,224},{224... | collective-permute-start | bytes 98312 | tf_op jit(solution)/shard_map/while/body/eval_jaxpr/ppermute | solution.py:12
  370.1 11.9 %collective-permute-start = (f32[2,4096]{1,0:T(2,128)S(1)}, f32[2,4096]{1,0:T(2,128)S(1)}, u32[]{:S(2)}, u32[]{:S(2)}) collective-permute-start(f32[2,4096]{1,0:T(2,128)S(1)} %get-tuple-element.292), channel_id=1, source_target_pairs={{0,32},{32,64},{64,96},{96,128},{128,160},{160,192},{192,224},{224... | collective-permute-start | bytes 98312 | tf_op jit(solution)/shard_map/while/body/eval_jaxpr/ppermute | solution.py:12
  382.9 11.8 %collective-permute-start = (f32[2,4096]{1,0:T(2,128)S(1)}, f32[2,4096]{1,0:T(2,128)S(1)}, u32[]{:S(2)}, u32[]{:S(2)}) collective-permute-start(f32[2,4096]{1,0:T(2,128)S(1)} %get-tuple-element.292), channel_id=1, source_target_pairs={{0,32},{32,64},{64,96},{96,128},{128,160},{160,192},{192,224},{224... | collective-permute-start | bytes 98312 | tf_op jit(solution)/shard_map/while/body/eval_jaxpr/ppermute | solution.py:12
  395.6 12.2 %collective-permute-start = (f32[2,4096]{1,0:T(2,128)S(1)}, f32[2,4096]{1,0:T(2,128)S(1)}, u32[]{:S(2)}, u32[]{:S(2)}) collective-permute-start(f32[2,4096]{1,0:T(2,128)S(1)} %get-tuple-element.292), channel_id=1, source_target_pairs={{0,32},{32,64},{64,96},{96,128},{128,160},{160,192},{192,224},{224... | collective-permute-start | bytes 98312 | tf_op jit(solution)/shard_map/while/body/eval_jaxpr/ppermute | solution.py:12
  408.8 11.9 %collective-permute-start = (f32[2,4096]{1,0:T(2,128)S(1)}, f32[2,4096]{1,0:T(2,128)S(1)}, u32[]{:S(2)}, u32[]{:S(2)}) collective-permute-start(f32[2,4096]{1,0:T(2,128)S(1)} %get-tuple-element.292), channel_id=1, source_target_pairs={{0,32},{32,64},{64,96},{96,128},{128,160},{160,192},{192,224},{224... | collective-permute-start | bytes 98312 | tf_op jit(solution)/shard_map/while/body/eval_jaxpr/ppermute | solution.py:12
  421.7 11.9 %collective-permute-start = (f32[2,4096]{1,0:T(2,128)S(1)}, f32[2,4096]{1,0:T(2,128)S(1)}, u32[]{:S(2)}, u32[]{:S(2)}) collective-permute-start(f32[2,4096]{1,0:T(2,128)S(1)} %get-tuple-element.292), channel_id=1, source_target_pairs={{0,32},{32,64},{64,96},{96,128},{128,160},{160,192},{192,224},{224... | collective-permute-start | bytes 98312 | tf_op jit(solution)/shard_map/while/body/eval_jaxpr/ppermute | solution.py:12
  434.4 11.9 %collective-permute-start = (f32[2,4096]{1,0:T(2,128)S(1)}, f32[2,4096]{1,0:T(2,128)S(1)}, u32[]{:S(2)}, u32[]{:S(2)}) collective-permute-start(f32[2,4096]{1,0:T(2,128)S(1)} %get-tuple-element.292), channel_id=1, source_target_pairs={{0,32},{32,64},{64,96},{96,128},{128,160},{160,192},{192,224},{224... | collective-permute-start | bytes 98312 | tf_op jit(solution)/shard_map/while/body/eval_jaxpr/ppermute | solution.py:12
  447.3 11.8 %collective-permute-start = (f32[2,4096]{1,0:T(2,128)S(1)}, f32[2,4096]{1,0:T(2,128)S(1)}, u32[]{:S(2)}, u32[]{:S(2)}) collective-permute-start(f32[2,4096]{1,0:T(2,128)S(1)} %get-tuple-element.292), channel_id=1, source_target_pairs={{0,32},{32,64},{64,96},{96,128},{128,160},{160,192},{192,224},{224... | collective-permute-start | bytes 98312 | tf_op jit(solution)/shard_map/while/body/eval_jaxpr/ppermute | solution.py:12
  460.0 11.8 %collective-permute-start = (f32[2,4096]{1,0:T(2,128)S(1)}, f32[2,4096]{1,0:T(2,128)S(1)}, u32[]{:S(2)}, u32[]{:S(2)}) collective-permute-start(f32[2,4096]{1,0:T(2,128)S(1)} %get-tuple-element.292), channel_id=1, source_target_pairs={{0,32},{32,64},{64,96},{96,128},{128,160},{160,192},{192,224},{224... | collective-permute-start | bytes 98312 | tf_op jit(solution)/shard_map/while/body/eval_jaxpr/ppermute | solution.py:12
  472.8 11.8 %collective-permute-start = (f32[2,4096]{1,0:T(2,128)S(1)}, f32[2,4096]{1,0:T(2,128)S(1)}, u32[]{:S(2)}, u32[]{:S(2)}) collective-permute-start(f32[2,4096]{1,0:T(2,128)S(1)} %get-tuple-element.292), channel_id=1, source_target_pairs={{0,32},{32,64},{64,96},{96,128},{128,160},{160,192},{192,224},{224... | collective-permute-start | bytes 98312 | tf_op jit(solution)/shard_map/while/body/eval_jaxpr/ppermute | solution.py:12
  485.6 11.8 %collective-permute-start = (f32[2,4096]{1,0:T(2,128)S(1)}, f32[2,4096]{1,0:T(2,128)S(1)}, u32[]{:S(2)}, u32[]{:S(2)}) collective-permute-start(f32[2,4096]{1,0:T(2,128)S(1)} %get-tuple-element.292), channel_id=1, source_target_pairs={{0,32},{32,64},{64,96},{96,128},{128,160},{160,192},{192,224},{224... | collective-permute-start | bytes 98312 | tf_op jit(solution)/shard_map/while/body/eval_jaxpr/ppermute | solution.py:12
  498.3 11.8 %collective-permute-start = (f32[2,4096]{1,0:T(2,128)S(1)}, f32[2,4096]{1,0:T(2,128)S(1)}, u32[]{:S(2)}, u32[]{:S(2)}) collective-permute-start(f32[2,4096]{1,0:T(2,128)S(1)} %get-tuple-element.292), channel_id=1, source_target_pairs={{0,32},{32,64},{64,96},{96,128},{128,160},{160,192},{192,224},{224... | collective-permute-start | bytes 98312 | tf_op jit(solution)/shard_map/while/body/eval_jaxpr/ppermute | solution.py:12
  511.1 0.6 copy-start.1
Sparse Core Ops, SparseCore 0:
  13.9 293.0 all-reduce.1
where the time goes:
time: 519 us
  waiting for transfers between devices  411 us (79%)
  starting transfers between devices  30.3 us (6%)
  matrix products  25.5 us (5%)
  loops' own time  20 us (4%)
  between operations  13.5 us (3%)
  other arithmetic  12.9 us (2%)
    psum x1, waiting for transfers between devices, body(): summed = lax.psum(partial_value, 'tensor')  292 us
    ppermute x15, waiting for transfers between devices, from_behind(): return lax.ppermute(value, axis, pairs)  119 us
    ppermute x15, starting transfers between devices, from_behind(): return lax.ppermute(value, axis, pairs)  30.3 us
    another operation x1, loops' own time, body(): _, result = lax.fori_loop(1, groups, advance, (mine, result))  20 us
    dot_general x16, matrix products, inner_rows(): lax.dot_general(left, right, (((1,), (1,)), ((), ())), preferred_element_...  14.8 us
    reduce_sum x15, other arithmetic, place(): source_task = jnp.sum(jnp.where(block_ids == source, task_ids, 0))  10.7 us
  transfers between devices with their start and end apart: 16, of which 16 were waited for; matrix products, arithmetic and copies ran while one was open for 2% of the time, Pallas kernels for 0%

commit v1 on v0

--- a/solution.py
+++ b/solution.py
@@ -54,7 +54,7 @@
     partial_value = jnp.concatenate([inputs_part, outputs_part], axis=1).reshape(
         block_rows, seq_len, 2 * width_low
     )
-    summed = lax.psum(partial_value, "tensor")
+    summed = jnp.sum(lax.all_gather(partial_value, "tensor"), axis=0)
     own_block = normalized(summed, lengths)
     mine = lax.dynamic_slice_in_dim(own_block, slice_index * share_rows, share_rows, 0)
     block_ids = jnp.arange(groups, dtype=jnp.int32)

time: 519 us -> 431 us (0.83)
  the two profiles are of different devices: /device:TPU:128 before, /device:TPU:226 now
where the time goes in v1:
time: 431 us
  waiting for transfers between devices  313 us (73%)
  starting transfers between devices  30.3 us (7%)
  matrix products  25.2 us (6%)
  other arithmetic  23.9 us (6%)
  loops' own time  19.5 us (5%)
  between operations  13.5 us (3%)
  local copies, waits for them, and re-layouts  5.38 us (1%)
    all_gather x1, waiting for transfers between devices, body(): summed = jnp.sum(lax.all_gather(partial_value, 'tensor'), axis=0)  191 us
    ppermute x15, waiting for transfers between devices, from_behind(): return lax.ppermute(value, axis, pairs)  122 us
    ppermute x15, starting transfers between devices, from_behind(): return lax.ppermute(value, axis, pairs)  30.3 us
    another operation x1, loops' own time, body(): _, result = lax.fori_loop(1, groups, advance, (mine, result))  19.5 us
    dot_general x16, matrix products, inner_rows(): lax.dot_general(left, right, (((1,), (1,)), ((), ())), preferred_element_...  14.8 us
    reduce_sum x1, other arithmetic, body(): summed = jnp.sum(lax.all_gather(partial_value, 'tensor'), axis=0)  12.3 us
    reduce_sum x15, other arithmetic, place(): source_task = jnp.sum(jnp.where(block_ids == source, task_ids, 0))  10.7 us
  transfers between devices with their start and end apart: 16, of which 16 were waited for; matrix products, arithmetic and copies ran while one was open for 3% of the time, Pallas kernels for 0%

profile of v1, /device:TPU:226, one launch (start us, length us, event | category | flops | bytes accessed | tf_op | source)
XLA Modules:
  0.0 430.5 jit_solution(7104620938526733610)
XLA Ops:
  8.9 3.3 fusion.13
  14.4 190.5 %all-gather.2.cloned.1.call-done = f32[32,64,32,128]{3,2,1,0:T(8,128)} async-done(((f32[1,64,32,128]{3,2,1,0:T(8,128)}), f32[32,64,32,128]{3,2,1,0:T(8,128)}) %all-gather.2.cloned.1.call-update) | async-done | bytes 33554448 | tf_op jit(solution)/shard_map/all_gather | solution.py:57
  204.9 12.3 %reduce_sum.47 = f32[64,32,128]{2,1,0:T(8,128)S(1)} reduce(f32[32,64,32,128]{3,2,1,0:T(8,128)} %all-gather.2.cloned.1.call-done, f32[]{:T(128)} %constant.84.clone.1), dimensions={0}, to_apply=%region_0.0 | reduce | flops 8126464 | bytes 34603012 | tf_op jit(solution)/shard_map/reduce_sum | solution.py:57
  217.2 5.9 %multiply_reduce_fusion = (f32[64]{0:T(128)S(1)}, f32[64,64,64]{2,1,0:T(8,128)}) fusion(f32[64,32,128]{2,1,0:T(8,128)S(1)} %reduce_sum.47, f32[64,32]{1,0:T(8,128)S(1)} %fusion.11), kind=kOutput, calls=%fused_computation.7 | convolution fusion | flops 101318592 | bytes 3178752 | tf_op jit(solution)/shard_map/slk,slm->skm/dot_general | solution.py:23
  223.1 2.1 reshape.41
  226.4 196.6 %while.18 = (s32[]{:T(128)}, f32[2,4096]{1,0:T(2,128)S(1)}, f32[64,16,2]{0,2,1:T(2,128)S(1)}, s32[]{:T(128)}, s32[16]{0:T(128)S(1)}, /*index=5*/s32[]{:T(128)}, ...) while((s32[]{:T(128)}, f32[2,4096]{1,0:T(2,128)S(1)}, ...), condition=%wide.region_5.6_spmd.clone, body=%wide.region_3.0_spmd.clone.sunk | while | flops 6291777 | bytes 1279366 | solution.py:79
  226.4 3.4 collective-permute-start
  231.8 7.9 %collective-permute-done = f32[2,4096]{1,0:T(2,128)S(1)} collective-permute-done((f32[2,4096]{1,0:T(2,128)S(1)}, f32[2,4096]{1,0:T(2,128)S(1)}, u32[]{:S(2)}, u32[]{:S(2)}) %collective-permute-start) | collective-permute-done | bytes 32800 | tf_op jit(solution)/shard_map/while/body/eval_jaxpr/ppermute | solution.py:12
  240.6 1.9 collective-permute-start
  244.6 8.7 %collective-permute-done = f32[2,4096]{1,0:T(2,128)S(1)} collective-permute-done((f32[2,4096]{1,0:T(2,128)S(1)}, f32[2,4096]{1,0:T(2,128)S(1)}, u32[]{:S(2)}, u32[]{:S(2)}) %collective-permute-start) | collective-permute-done | bytes 32800 | tf_op jit(solution)/shard_map/while/body/eval_jaxpr/ppermute | solution.py:12
  254.2 1.9 collective-permute-start
  258.1 8.3 %collective-permute-done = f32[2,4096]{1,0:T(2,128)S(1)} collective-permute-done((f32[2,4096]{1,0:T(2,128)S(1)}, f32[2,4096]{1,0:T(2,128)S(1)}, u32[]{:S(2)}, u32[]{:S(2)}) %collective-permute-start) | collective-permute-done | bytes 32800 | tf_op jit(solution)/shard_map/while/body/eval_jaxpr/ppermute | solution.py:12
  271.3 8.0 %collective-permute-done = f32[2,4096]{1,0:T(2,128)S(1)} collective-permute-done((f32[2,4096]{1,0:T(2,128)S(1)}, f32[2,4096]{1,0:T(2,128)S(1)}, u32[]{:S(2)}, u32[]{:S(2)}) %collective-permute-start) | collective-permute-done | bytes 32800 | tf_op jit(solution)/shard_map/while/body/eval_jaxpr/ppermute | solution.py:12
  284.1 7.9 %collective-permute-done = f32[2,4096]{1,0:T(2,128)S(1)} collective-permute-done((f32[2,4096]{1,0:T(2,128)S(1)}, f32[2,4096]{1,0:T(2,128)S(1)}, u32[]{:S(2)}, u32[]{:S(2)}) %collective-permute-start) | collective-permute-done | bytes 32800 | tf_op jit(solution)/shard_map/while/body/eval_jaxpr/ppermute | solution.py:12
  296.9 7.9 %collective-permute-done = f32[2,4096]{1,0:T(2,128)S(1)} collective-permute-done((f32[2,4096]{1,0:T(2,128)S(1)}, f32[2,4096]{1,0:T(2,128)S(1)}, u32[]{:S(2)}, u32[]{:S(2)}) %collective-permute-start) | collective-permute-done | bytes 32800 | tf_op jit(solution)/shard_map/while/body/eval_jaxpr/ppermute | solution.py:12
  309.7 8.0 %collective-permute-done = f32[2,4096]{1,0:T(2,128)S(1)} collective-permute-done((f32[2,4096]{1,0:T(2,128)S(1)}, f32[2,4096]{1,0:T(2,128)S(1)}, u32[]{:S(2)}, u32[]{:S(2)}) %collective-permute-start) | collective-permute-done | bytes 32800 | tf_op jit(solution)/shard_map/while/body/eval_jaxpr/ppermute | solution.py:12
  322.5 7.9 %collective-permute-done = f32[2,4096]{1,0:T(2,128)S(1)} collective-permute-done((f32[2,4096]{1,0:T(2,128)S(1)}, f32[2,4096]{1,0:T(2,128)S(1)}, u32[]{:S(2)}, u32[]{:S(2)}) %collective-permute-start) | collective-permute-done | bytes 32800 | tf_op jit(solution)/shard_map/while/body/eval_jaxpr/ppermute | solution.py:12
  335.3 8.1 %collective-permute-done = f32[2,4096]{1,0:T(2,128)S(1)} collective-permute-done((f32[2,4096]{1,0:T(2,128)S(1)}, f32[2,4096]{1,0:T(2,128)S(1)}, u32[]{:S(2)}, u32[]{:S(2)}) %collective-permute-start) | collective-permute-done | bytes 32800 | tf_op jit(solution)/shard_map/while/body/eval_jaxpr/ppermute | solution.py:12
  348.2 9.2 %collective-permute-done = f32[2,4096]{1,0:T(2,128)S(1)} collective-permute-done((f32[2,4096]{1,0:T(2,128)S(1)}, f32[2,4096]{1,0:T(2,128)S(1)}, u32[]{:S(2)}, u32[]{:S(2)}) %collective-permute-start) | collective-permute-done | bytes 32800 | tf_op jit(solution)/shard_map/while/body/eval_jaxpr/ppermute | solution.py:12
  362.3 8.4 %collective-permute-done = f32[2,4096]{1,0:T(2,128)S(1)} collective-permute-done((f32[2,4096]{1,0:T(2,128)S(1)}, f32[2,4096]{1,0:T(2,128)S(1)}, u32[]{:S(2)}, u32[]{:S(2)}) %collective-permute-start) | collective-permute-done | bytes 32800 | tf_op jit(solution)/shard_map/while/body/eval_jaxpr/ppermute | solution.py:12
  375.6 8.3 %collective-permute-done = f32[2,4096]{1,0:T(2,128)S(1)} collective-permute-done((f32[2,4096]{1,0:T(2,128)S(1)}, f32[2,4096]{1,0:T(2,128)S(1)}, u32[]{:S(2)}, u32[]{:S(2)}) %collective-permute-start) | collective-permute-done | bytes 32800 | tf_op jit(solution)/shard_map/while/body/eval_jaxpr/ppermute | solution.py:12
  388.7 7.9 %collective-permute-done = f32[2,4096]{1,0:T(2,128)S(1)} collective-permute-done((f32[2,4096]{1,0:T(2,128)S(1)}, f32[2,4096]{1,0:T(2,128)S(1)}, u32[]{:S(2)}, u32[]{:S(2)}) %collective-permute-start) | collective-permute-done | bytes 32800 | tf_op jit(solution)/shard_map/while/body/eval_jaxpr/ppermute | solution.py:12
  401.5 7.9 %collective-permute-done = f32[2,4096]{1,0:T(2,128)S(1)} collective-permute-done((f32[2,4096]{1,0:T(2,128)S(1)}, f32[2,4096]{1,0:T(2,128)S(1)}, u32[]{:S(2)}, u32[]{:S(2)}) %collective-permute-start) | collective-permute-done | bytes 32800 | tf_op jit(solution)/shard_map/while/body/eval_jaxpr/ppermute | solution.py:12
  414.2 7.9 %collective-permute-done = f32[2,4096]{1,0:T(2,128)S(1)} collective-permute-done((f32[2,4096]{1,0:T(2,128)S(1)}, f32[2,4096]{1,0:T(2,128)S(1)}, u32[]{:S(2)}, u32[]{:S(2)}) %collective-permute-start) | collective-permute-done | bytes 32800 | tf_op jit(solution)/shard_map/while/body/eval_jaxpr/ppermute | solution.py:12
  (77 shorter events, 54.0 us)
Async XLA Ops:
  6.5 1.2 copy-start
  6.5 198.4 %all-gather.2.cloned.1.call-start = ((), (), s32[]{:S(2)}) async-start(), calls=%async_computation | async-start | bytes 34603008 | tf_op jit(solution)/shard_map/all_gather | solution.py:57
  12.2 1.5 copy-start.3
  12.2 2.1 copy-start.2
  226.4 13.3 %collective-permute-start = (f32[2,4096]{1,0:T(2,128)S(1)}, f32[2,4096]{1,0:T(2,128)S(1)}, u32[]{:S(2)}, u32[]{:S(2)}) collective-permute-start(f32[2,4096]{1,0:T(2,128)S(1)} %get-tuple-element.292), channel_id=1, source_target_pairs={{0,32},{32,64},{64,96},{96,128},{128,160},{160,192},{192,224},{224... | collective-permute-start | bytes 98312 | tf_op jit(solution)/shard_map/while/body/eval_jaxpr/ppermute | solution.py:12
  240.6 12.6 %collective-permute-start = (f32[2,4096]{1,0:T(2,128)S(1)}, f32[2,4096]{1,0:T(2,128)S(1)}, u32[]{:S(2)}, u32[]{:S(2)}) collective-permute-start(f32[2,4096]{1,0:T(2,128)S(1)} %get-tuple-element.292), channel_id=1, source_target_pairs={{0,32},{32,64},{64,96},{96,128},{128,160},{160,192},{192,224},{224... | collective-permute-start | bytes 98312 | tf_op jit(solution)/shard_map/while/body/eval_jaxpr/ppermute | solution.py:12
  254.2 12.3 %collective-permute-start = (f32[2,4096]{1,0:T(2,128)S(1)}, f32[2,4096]{1,0:T(2,128)S(1)}, u32[]{:S(2)}, u32[]{:S(2)}) collective-permute-start(f32[2,4096]{1,0:T(2,128)S(1)} %get-tuple-element.292), channel_id=1, source_target_pairs={{0,32},{32,64},{64,96},{96,128},{128,160},{160,192},{192,224},{224... | collective-permute-start | bytes 98312 | tf_op jit(solution)/shard_map/while/body/eval_jaxpr/ppermute | solution.py:12
  267.4 11.9 %collective-permute-start = (f32[2,4096]{1,0:T(2,128)S(1)}, f32[2,4096]{1,0:T(2,128)S(1)}, u32[]{:S(2)}, u32[]{:S(2)}) collective-permute-start(f32[2,4096]{1,0:T(2,128)S(1)} %get-tuple-element.292), channel_id=1, source_target_pairs={{0,32},{32,64},{64,96},{96,128},{128,160},{160,192},{192,224},{224... | collective-permute-start | bytes 98312 | tf_op jit(solution)/shard_map/while/body/eval_jaxpr/ppermute | solution.py:12
  280.2 11.9 %collective-permute-start = (f32[2,4096]{1,0:T(2,128)S(1)}, f32[2,4096]{1,0:T(2,128)S(1)}, u32[]{:S(2)}, u32[]{:S(2)}) collective-permute-start(f32[2,4096]{1,0:T(2,128)S(1)} %get-tuple-element.292), channel_id=1, source_target_pairs={{0,32},{32,64},{64,96},{96,128},{128,160},{160,192},{192,224},{224... | collective-permute-start | bytes 98312 | tf_op jit(solution)/shard_map/while/body/eval_jaxpr/ppermute | solution.py:12
  293.0 11.8 %collective-permute-start = (f32[2,4096]{1,0:T(2,128)S(1)}, f32[2,4096]{1,0:T(2,128)S(1)}, u32[]{:S(2)}, u32[]{:S(2)}) collective-permute-start(f32[2,4096]{1,0:T(2,128)S(1)} %get-tuple-element.292), channel_id=1, source_target_pairs={{0,32},{32,64},{64,96},{96,128},{128,160},{160,192},{192,224},{224... | collective-permute-start | bytes 98312 | tf_op jit(solution)/shard_map/while/body/eval_jaxpr/ppermute | solution.py:12
  305.7 11.9 %collective-permute-start = (f32[2,4096]{1,0:T(2,128)S(1)}, f32[2,4096]{1,0:T(2,128)S(1)}, u32[]{:S(2)}, u32[]{:S(2)}) collective-permute-start(f32[2,4096]{1,0:T(2,128)S(1)} %get-tuple-element.292), channel_id=1, source_target_pairs={{0,32},{32,64},{64,96},{96,128},{128,160},{160,192},{192,224},{224... | collective-permute-start | bytes 98312 | tf_op jit(solution)/shard_map/while/body/eval_jaxpr/ppermute | solution.py:12
  318.6 11.9 %collective-permute-start = (f32[2,4096]{1,0:T(2,128)S(1)}, f32[2,4096]{1,0:T(2,128)S(1)}, u32[]{:S(2)}, u32[]{:S(2)}) collective-permute-start(f32[2,4096]{1,0:T(2,128)S(1)} %get-tuple-element.292), channel_id=1, source_target_pairs={{0,32},{32,64},{64,96},{96,128},{128,160},{160,192},{192,224},{224... | collective-permute-start | bytes 98312 | tf_op jit(solution)/shard_map/while/body/eval_jaxpr/ppermute | solution.py:12
  331.3 12.0 %collective-permute-start = (f32[2,4096]{1,0:T(2,128)S(1)}, f32[2,4096]{1,0:T(2,128)S(1)}, u32[]{:S(2)}, u32[]{:S(2)}) collective-permute-start(f32[2,4096]{1,0:T(2,128)S(1)} %get-tuple-element.292), channel_id=1, source_target_pairs={{0,32},{32,64},{64,96},{96,128},{128,160},{160,192},{192,224},{224... | collective-permute-start | bytes 98312 | tf_op jit(solution)/shard_map/while/body/eval_jaxpr/ppermute | solution.py:12
  344.3 13.1 %collective-permute-start = (f32[2,4096]{1,0:T(2,128)S(1)}, f32[2,4096]{1,0:T(2,128)S(1)}, u32[]{:S(2)}, u32[]{:S(2)}) collective-permute-start(f32[2,4096]{1,0:T(2,128)S(1)} %get-tuple-element.292), channel_id=1, source_target_pairs={{0,32},{32,64},{64,96},{96,128},{128,160},{160,192},{192,224},{224... | collective-permute-start | bytes 98312 | tf_op jit(solution)/shard_map/while/body/eval_jaxpr/ppermute | solution.py:12
  358.4 12.4 %collective-permute-start = (f32[2,4096]{1,0:T(2,128)S(1)}, f32[2,4096]{1,0:T(2,128)S(1)}, u32[]{:S(2)}, u32[]{:S(2)}) collective-permute-start(f32[2,4096]{1,0:T(2,128)S(1)} %get-tuple-element.292), channel_id=1, source_target_pairs={{0,32},{32,64},{64,96},{96,128},{128,160},{160,192},{192,224},{224... | collective-permute-start | bytes 98312 | tf_op jit(solution)/shard_map/while/body/eval_jaxpr/ppermute | solution.py:12
  371.6 12.2 %collective-permute-start = (f32[2,4096]{1,0:T(2,128)S(1)}, f32[2,4096]{1,0:T(2,128)S(1)}, u32[]{:S(2)}, u32[]{:S(2)}) collective-permute-start(f32[2,4096]{1,0:T(2,128)S(1)} %get-tuple-element.292), channel_id=1, source_target_pairs={{0,32},{32,64},{64,96},{96,128},{128,160},{160,192},{192,224},{224... | collective-permute-start | bytes 98312 | tf_op jit(solution)/shard_map/while/body/eval_jaxpr/ppermute | solution.py:12
  384.8 11.8 %collective-permute-start = (f32[2,4096]{1,0:T(2,128)S(1)}, f32[2,4096]{1,0:T(2,128)S(1)}, u32[]{:S(2)}, u32[]{:S(2)}) collective-permute-start(f32[2,4096]{1,0:T(2,128)S(1)} %get-tuple-element.292), channel_id=1, source_target_pairs={{0,32},{32,64},{64,96},{96,128},{128,160},{160,192},{192,224},{224... | collective-permute-start | bytes 98312 | tf_op jit(solution)/shard_map/while/body/eval_jaxpr/ppermute | solution.py:12
  397.5 11.8 %collective-permute-start = (f32[2,4096]{1,0:T(2,128)S(1)}, f32[2,4096]{1,0:T(2,128)S(1)}, u32[]{:S(2)}, u32[]{:S(2)}) collective-permute-start(f32[2,4096]{1,0:T(2,128)S(1)} %get-tuple-element.292), channel_id=1, source_target_pairs={{0,32},{32,64},{64,96},{96,128},{128,160},{160,192},{192,224},{224... | collective-permute-start | bytes 98312 | tf_op jit(solution)/shard_map/while/body/eval_jaxpr/ppermute | solution.py:12
  410.3 11.8 %collective-permute-start = (f32[2,4096]{1,0:T(2,128)S(1)}, f32[2,4096]{1,0:T(2,128)S(1)}, u32[]{:S(2)}, u32[]{:S(2)}) collective-permute-start(f32[2,4096]{1,0:T(2,128)S(1)} %get-tuple-element.292), channel_id=1, source_target_pairs={{0,32},{32,64},{64,96},{96,128},{128,160},{160,192},{192,224},{224... | collective-permute-start | bytes 98312 | tf_op jit(solution)/shard_map/while/body/eval_jaxpr/ppermute | solution.py:12
  423.0 0.6 copy-start.1
Sparse Core Ops, SparseCore 0:
  13.8 191.0 all-gather.1
